TPU v7x, 256 devices: a whole 4x4x8 slice. The times are simulated.
256 devices in a mesh: seq: 32 (over y, z), tp: 8 (over x, core).
Axes of the slice: x: 4, y: 4, z: 8, core: 2. Of those that a mesh axis runs over, the one named last changes fastest.
Arguments:
- tokens: bfloat16 [16384, 4096], P('seq', 'tp'), may hold values from -40 to 40, as said below
- w_query: bfloat16 [4096, 2048], P(None, 'tp'), may hold values from -0.09375 to 0.09375
- w_key: bfloat16 [4096, 2048], P(None, 'tp'), may hold values from -0.09375 to 0.09375
- w_value: bfloat16 [4096, 2048], P(None, 'tp'), may hold values from -0.09375 to 0.09375
- w_gate: bfloat16 [4096, 2048], P(None, 'tp'), may hold values from -0.09375 to 0.09375
- w_out: bfloat16 [2048, 4096], P(None, 'tp'), may hold values from -0.125 to 0.125
- decay_rate: float32 [16], replicated, may hold values from 1.8310547e-05 to 0.0333333333, as said below
- state_in: float32 [16, 128, 128], P('tp'), may hold values from -192 to 192
Outputs:
- layer_out: bfloat16 [16384, 4096], P('seq', 'tp')
Inputs may be any that keep to these rules, and one draw needn't show every extreme that they name: tokens have scales that vary by row and by column. `decay_rate`: each head either forgets within a few tens of positions or keeps its state over the whole slab.
All inputs are finite; a program needn't handle non-finite values.
Results may differ from a plain program's by a relative error of at most 0.0033.
Values may be sent and summed in bfloat16 or wider, within the bound.
A program may use at most 64 MiB of HBM per device.

v0:
```python
import jax
import jax.numpy as jnp
from jax import lax
from jax.sharding import PartitionSpec as P


def per_device(tokens, w_query, w_key, w_value, w_gate, w_out, decay_rate, state_in):
    hi = lax.Precision.HIGHEST
    row_count = tokens.shape[0]
    width_all = w_query.shape[0]
    heads_here = state_in.shape[0]
    head_dim = state_in.shape[1]
    tp_index = lax.axis_index("tp")
    seq_index = lax.axis_index("seq")
    weight_set = (w_query, w_key, w_value, w_gate)
    gathered = lax.all_gather(tokens, "tp", axis=1, tiled=True)
    gathered_f = gathered.astype(jnp.float32)
    square_sum = jnp.sum(gathered_f * gathered_f, axis=1, keepdims=True)
    raw_set = tuple(
        (jnp.dot(gathered, weight, preferred_element_type=jnp.float32) for weight in weight_set)
    )
    inv_rms = lax.rsqrt(square_sum / float(width_all) + 1e-06)

    def to_heads(array):
        return array.reshape(row_count, heads_here, head_dim).transpose(1, 0, 2)

    query_h = to_heads(jax.nn.silu(raw_set[0] * inv_rms).astype(jnp.bfloat16))
    key_h = to_heads(jax.nn.silu(raw_set[1] * inv_rms).astype(jnp.bfloat16))
    value_h = to_heads((raw_set[2] * inv_rms).astype(jnp.bfloat16))
    gate = jax.nn.silu(raw_set[3] * inv_rms)
    rate_here = lax.dynamic_slice_in_dim(decay_rate, tp_index * heads_here, heads_here)
    rate_col = rate_here[:, None]
    positions = jnp.arange(row_count).astype(jnp.float32)
    lower = positions[:, None] >= positions[None, :]
    gap_mask = jnp.where(lower, positions[:, None] - positions[None, :], 0.0)
    scores = jnp.einsum("hid,hjd->hij", query_h, key_h, preferred_element_type=jnp.float32)
    mask = jnp.where(lower[None], jnp.exp(-rate_col[:, :, None] * gap_mask[None]), 0.0)
    weights = (scores * mask).astype(jnp.bfloat16)
    intra = jnp.einsum("hij,hje->hie", weights, value_h, preferred_element_type=jnp.float32)
    value_f = value_h.astype(jnp.float32)
    tail_decay = jnp.exp(-rate_col * (row_count - 1.0 - positions[None, :]))
    local_state = jnp.einsum(
        "hid,hie->hde", key_h.astype(jnp.float32) * tail_decay[:, :, None], value_f, precision=hi
    )
    piece = lax.all_gather(
        local_state[None].astype(jnp.bfloat16), "seq", axis=0, tiled=True
    ).astype(jnp.float32)
    count = piece.shape[0]
    source = jnp.arange(count)
    distance = seq_index - 1 - source
    exponent = (row_count * jnp.maximum(distance, 0)).astype(jnp.float32)
    factor = jnp.where(
        distance[:, None] >= 0, jnp.exp(-rate_here[None, :] * exponent[:, None]), 0.0
    )
    prefix = jnp.zeros_like(local_state) + jnp.sum(factor[:, :, None, None] * piece, axis=0)
    offset = (row_count * seq_index).astype(jnp.float32)
    incoming = prefix + jnp.exp(-rate_here * offset)[:, None, None] * state_in
    lead_decay = jnp.exp(-rate_col * (positions[None, :] + 1.0))
    inter = jnp.einsum(
        "hid,hde->hie", query_h.astype(jnp.float32) * lead_decay[:, :, None], incoming, precision=hi
    )
    attended = intra + inter
    norm_inv = lax.rsqrt(jnp.mean(attended * attended, axis=2, keepdims=True) + 1e-06)
    normed = (attended * norm_inv).transpose(1, 0, 2).reshape(row_count, heads_here * head_dim)
    hidden = (normed * gate).astype(jnp.bfloat16)
    branch = jnp.dot(
        lax.all_gather(hidden, "tp", axis=1, tiled=True), w_out, preferred_element_type=jnp.float32
    )
    return (tokens.astype(jnp.float32) + branch).astype(jnp.bfloat16)


def solution(mesh):
    return jax.shard_map(
        per_device,
        mesh=mesh,
        in_specs=(
            P("seq", "tp"),
            P(None, "tp"),
            P(None, "tp"),
            P(None, "tp"),
            P(None, "tp"),
            P(None, "tp"),
            P(),
            P("tp", None, None),
        ),
        out_specs=P("seq", "tp"),
        check_vma=False,
    )
```

profile of v0, /device:TPU:1, one launch (start us, length us, event | category | flops | bytes accessed | tf_op | source)
XLA Modules:
  0.0 186.8 jit_solution(16274440902370304356)
XLA Ops:
  6.5 0.7 all-gather.5.cloned.1.call-update
  7.3 1.3 multiply_exponential_fusion.2
  8.6 0.7 multiply_exponential_fusion
  9.3 38.8 %all-gather.5.cloned.1.call-done = bf16[512,4096]{1,0:T(8,128)(2,1)} async-done(((bf16[512,512]{1,0:T(8,128)(2,1)}), bf16[512,4096]{1,0:T(8,128)(2,1)}) %all-gather.5.cloned.1.call-update) | async-done | bytes 4194320 | tf_op jit(solution)/shard_map/all_gather | solution.py:16
  48.1 3.2 %multiply_reduce_fusion = f32[512]{0:T(512)S(1)} fusion(bf16[512,4096]{1,0:T(8,128)(2,1)} %all-gather.5.cloned.1.call-done), kind=kLoop, calls=%fused_computation | loop fusion | flops 6290944 | bytes 4196352 | tf_op jit(solution)/shard_map/reduce_sum | solution.py:18
  51.3 0.2 copy-done.1
  51.5 2.9 %fusion.4 = bf16[512,256]{0,1:T(8,128)(2,1)S(1)} fusion(bf16[512,4096]{1,0:T(8,128)(2,1)S(1)} %copy-done.1, bf16[4096,256]{1,0:T(8,128)(2,1)} %param.11, f32[512]{0:T(512)S(1)} %add_rsqrt_fusion), kind=kOutput, calls=%fused_computation.12 | convolution fusion | flops 1074003968 | bytes 6555648 | tf_op jit(solution)/shard_map/dot_general | solution.py:20
  54.5 0.2 copy.15
  54.6 4.2 %multiply_convert_fusion.1 = bf16[512,256]{0,1:T(8,128)(2,1)S(1)} fusion(bf16[512,4096]{1,0:T(8,128)(2,1)} %all-gather.5.cloned.1.call-done, bf16[4096,256]{1,0:T(8,128)(2,1)} %param.10, f32[512]{0:T(512)S(1)} %add_rsqrt_fusion), kind=kOutput, calls=%fused_computation.29 | convolution fusion | flops 1074528256 | bytes 6555648 | tf_op jit(solution)/shard_map/dot_general | solution.py:20
  58.9 0.7 copy-done.3
  59.6 1.0 convolution_convert_fusion
  60.8 0.1 exponential_select_fusion
  60.9 0.9 broadcast_compare_fusion
  61.8 0.2 subtract_select_fusion
  62.0 5.0 %multiply_convert_fusion.2 = bf16[512,256]{0,1:T(8,128)(2,1)} fusion(bf16[512,4096]{1,0:T(8,128)(2,1)} %all-gather.5.cloned.1.call-done, bf16[4096,256]{1,0:T(8,128)(2,1)} %param.9, f32[512]{0:T(512)S(1)} %add_rsqrt_fusion), kind=kOutput, calls=%fused_computation.30 | convolution fusion | flops 1074528256 | bytes 6555648 | tf_op jit(solution)/shard_map/dot_general | solution.py:20
  66.9 1.2 copy.14
  68.1 66.4 %all-gather.9.cloned.1.call-done = bf16[64,128,128]{2,1,0:T(8,128)(2,1)} async-done(((bf16[2,128,128]{2,1,0:T(8,128)(2,1)}), bf16[64,128,128]{2,1,0:T(8,128)(2,1)}) %all-gather.9.cloned.1.call-update) | async-done | bytes 2097168 | tf_op jit(solution)/shard_map/all_gather | solution.py:45
  134.5 2.1 %fusion = f32[2,128,128]{2,1,0:T(8,128)S(1)} fusion(bf16[32,2,128,128]{3,2,1,0:T(8,128)(2,1)} %bitcast.42, f32[32,2]{1,0:T(8,128)S(1)} %exponential_select_fusion), kind=kLoop, calls=%fused_computation.2 | loop fusion | flops 3112960 | bytes 2228480 | tf_op jit(solution)/shard_map/reduce_sum | solution.py:55
  136.6 1.6 fusion.12
  138.1 3.0 %multiply_reduce_fusion.1 = (f32[2,512]{1,0:T(2,128)S(1)}, f32[2,512,128]{1,2,0:T(8,128)}) fusion(f32[2,512,128]{1,2,0:T(8,128)} %fusion.12, bf16[2,512,128]{1,2,0:T(8,128)(2,1)} %bitcast.46, bf16[2,512,128]{1,2,0:T(8,128)(2,1)} %bitcast.44, f32[512,512]{1,0:T(8,128)S(1)} %subtract_select_fusion, f32[2]{0:T(128)} %copy-done.7, ...), kind=kOutput, calls=%fused_computation.22 | convolution fusion | flops 270924800 | bytes 3149832 | tf_op jit(solution)/shard_map/hij,hje->hie/dot_general | solution.py:39
  141.1 1.1 bitcast_multiply_fusion.1
  142.3 5.0 %fusion.9 = bf16[512,256]{0,1:T(8,128)(2,1)} fusion(f32[512,2,128]{0,2,1:T(8,128)S(1)} %bitcast_multiply_fusion.1, bf16[512,4096]{1,0:T(8,128)(2,1)} %all-gather.5.cloned.1.call-done, bf16[4096,256]{1,0:T(8,128)(2,1)} %param.12, f32[512]{0:T(512)S(1)} %copy-done.10), kind=kOutput, calls=%fused_computation.20 | convolution fusion | flops 1074659328 | bytes 7079936 | tf_op jit(solution)/shard_map/dot_general | solution.py:20
  147.3 29.4 %all-gather.7.cloned.1.call-done = bf16[512,2048]{0,1:T(8,128)(2,1)} async-done(((bf16[512,256]{0,1:T(8,128)(2,1)}), bf16[512,2048]{0,1:T(8,128)(2,1)}) %all-gather.7.cloned.1.call-update) | async-done | bytes 2097168 | tf_op jit(solution)/shard_map/all_gather | solution.py:67
  176.6 3.7 %fusion.2 = bf16[512,512]{1,0:T(8,128)(2,1)} fusion(bf16[512,2048]{0,1:T(8,128)(2,1)} %all-gather.7.cloned.1.call-done, bf16[2048,512]{1,0:T(8,128)(2,1)S(1)} %copy-done, bf16[512,512]{1,0:T(8,128)(2,1)S(1)} %copy-done.2), kind=kOutput, calls=%fused_computation.6 | convolution fusion | flops 1074528256 | bytes 5242880 | tf_op jit(solution)/shard_map/dot_general | solution.py:66
  (31 shorter events, 0.2 us)
Async XLA Ops:
  6.5 170.1 %copy-start = (bf16[2048,512]{1,0:T(8,128)(2,1)S(1)}, bf16[2048,512]{1,0:T(8,128)(2,1)}, u32[]{:S(2)}) copy-start(bf16[2048,512]{1,0:T(8,128)(2,1)} %param.13) | copy-start | bytes 6291460
  6.5 41.5 %all-gather.5.cloned.1.call-start = ((), (), s32[]{:S(2)}) async-start(), calls=%async_computation | async-start | bytes 4718592 | tf_op jit(solution)/shard_map/all_gather | solution.py:16
  7.3 127.2 %all-gather.9.cloned.1.call-start = ((), (), s32[]{:S(2)}) async-start(), calls=%async_computation.2 | async-start | bytes 2162688 | tf_op jit(solution)/shard_map/all_gather | solution.py:45
  8.6 52.2 %copy-start.7 = (f32[2]{0:T(128)}, f32[2]{0:T(128)S(1)}, u32[]{:S(2)}) copy-start(f32[2]{0:T(128)S(1)} %get-tuple-element.6) | copy-start | bytes 28
  48.1 3.4 %copy-start.1 = (bf16[512,4096]{1,0:T(8,128)(2,1)S(1)}, bf16[512,4096]{1,0:T(8,128)(2,1)}, u32[]{:S(2)}) copy-start(bf16[512,4096]{1,0:T(8,128)(2,1)} %all-gather.5.cloned.1.call-done) | copy-start | bytes 12582916
  51.5 10.4 %copy-start.9 = (f32[512]{0:T(512)}, f32[512]{0:T(512)S(1)}, u32[]{:S(2)}) copy-start(f32[512]{0:T(512)S(1)} %add_rsqrt_fusion) | copy-start | bytes 6148
  54.5 4.4 %copy-start.4 = (bf16[512,256]{0,1:T(8,128)(2,1)}, bf16[512,256]{0,1:T(8,128)(2,1)S(1)}, u32[]{:S(2)}) copy-start(bf16[512,256]{0,1:T(8,128)(2,1)S(1)} %fusion.4) | copy-start | bytes 786436
  58.9 0.7 copy-start.3
  60.7 116.0 %all-gather.7.cloned.1.call-start = ((), (), s32[]{:S(2)}) async-start(), calls=%async_computation.1 | async-start | bytes 2359296 | tf_op jit(solution)/shard_map/all_gather | solution.py:67
  66.9 69.6 %copy-start.5 = (f32[2,128,128]{2,1,0:T(8,128)S(1)}, f32[2,128,128]{2,1,0:T(8,128)}, u32[]{:S(2)}) copy-start(f32[2,128,128]{2,1,0:T(8,128)} %param.15) | copy-start | bytes 393220
  134.4 2.1 %copy-start.6 = (f32[2,512]{1,0:T(2,128)S(1)}, f32[2,512]{1,0:T(2,128)}, u32[]{:S(2)}) copy-start(f32[2,512]{1,0:T(2,128)} %get-tuple-element.8) | copy-start | bytes 12292
  134.4 2.1 %copy-start.8 = (f32[2]{0:T(128)S(1)}, f32[2]{0:T(128)}, u32[]{:S(2)}) copy-start(f32[2]{0:T(128)} %get-tuple-element.5) | copy-start | bytes 28
  138.1 4.1 %copy-start.10 = (f32[512]{0:T(512)S(1)}, f32[512]{0:T(512)}, u32[]{:S(2)}) copy-start(f32[512]{0:T(512)} %copy-done.9) | copy-start | bytes 6148
  142.2 34.4 %copy-start.2 = (bf16[512,512]{1,0:T(8,128)(2,1)S(1)}, bf16[512,512]{1,0:T(8,128)(2,1)}, u32[]{:S(2)}) copy-start(bf16[512,512]{1,0:T(8,128)(2,1)} %param.8) | copy-start | bytes 1572868
Sparse Core Ops, SparseCore 0:
  9.2 38.8 all-gather.4
  60.8 73.6 all-gather.8
  147.4 29.1 all-gather.6
where the time goes:
time: 187 us
  waiting for transfers between devices  135 us (72%)
  matrix products  26.3 us (14%)
  between operations  13.3 us (7%)
  other arithmetic  9.55 us (5%)
  local copies, waits for them, and re-layouts  2.27 us (1%)
    all_gather x1, waiting for transfers between devices, per_device(): lax.all_gather(local_state[None].astype(jnp.bfloat16), 'seq', axis=0, til...  66.4 us
    all_gather x1, waiting for transfers between devices, per_device(): gathered = lax.all_gather(tokens, 'tp', axis=1, tiled=True)  38.8 us
    all_gather x1, waiting for transfers between devices, per_device(): lax.all_gather(hidden, 'tp', axis=1, tiled=True)  29.4 us
    dot_general x4, matrix products, per_device(): jnp.dot(gathered, weight, preferred_element_type=jnp.float32)  17.1 us
  transfers between devices with their start and end apart: 3, of which 3 were waited for; matrix products, arithmetic and copies ran while one was open for 5% of the time, Pallas kernels for 0%

commit v1 on v0

--- a/solution.py
+++ b/solution.py
@@ -42,8 +42,14 @@
     local_state = jnp.einsum(
         "hid,hie->hde", key_h.astype(jnp.float32) * tail_decay[:, :, None], value_f, precision=hi
     )
-    piece = lax.all_gather(
-        local_state[None].astype(jnp.bfloat16), "seq", axis=0, tiled=True
+    piece = jnp.concatenate(
+        lax.all_to_all(
+            jnp.stack(lax.axis_size("seq") * [local_state[None].astype(jnp.bfloat16)], 0),
+            "seq",
+            0,
+            0,
+        ),
+        axis=0,
     ).astype(jnp.float32)
     count = piece.shape[0]
     source = jnp.arange(count)

time: 187 us -> 170 us (0.909)
  waiting for transfers between devices: 135 us -> 107 us
  starting transfers between devices: 0.08 us -> 9.74 us
    all_gather x1 -> x0, waiting for transfers between devices: 66.4 us -> none  [per_device(): lax.all_gather(local_state[None].astype(jnp.bfloat16), 'seq', axis=0, til...]
    all_to_all x0 -> x1, waiting for transfers between devices: none -> 41.5 us  [per_device(): lax.all_to_all(jnp.stack(lax.axis_size('seq') * [local_state[None].astype...]
    all_to_all x0 -> x1, starting transfers between devices: none -> 9.7 us  [per_device(): lax.all_to_all(jnp.stack(lax.axis_size('seq') * [local_state[None].astype...]
    all_gather x1, waiting for transfers between devices: 29.4 us -> 26.2 us  [per_device(): lax.all_gather(hidden, 'tp', axis=1, tiled=True)]
where the time goes in v1:
time: 170 us
  waiting for transfers between devices  107 us (63%)
  matrix products  25.7 us (15%)
  between operations  13.6 us (8%)
  starting transfers between devices  9.74 us (6%)
  other arithmetic  9.62 us (6%)
  local copies, waits for them, and re-layouts  3.73 us (2%)
    all_to_all x1, waiting for transfers between devices, per_device(): lax.all_to_all(jnp.stack(lax.axis_size('seq') * [local_state[None].astype...  41.5 us
    all_gather x1, waiting for transfers between devices, per_device(): gathered = lax.all_gather(tokens, 'tp', axis=1, tiled=True)  38.8 us
    all_gather x1, waiting for transfers between devices, per_device(): lax.all_gather(hidden, 'tp', axis=1, tiled=True)  26.2 us
    dot_general x4, matrix products, per_device(): jnp.dot(gathered, weight, preferred_element_type=jnp.float32)  17.1 us
    all_to_all x1, starting transfers between devices, per_device(): lax.all_to_all(jnp.stack(lax.axis_size('seq') * [local_state[None].astype...  9.7 us
    dot_general x1, matrix products, per_device(): jnp.dot(lax.all_gather(hidden, 'tp', axis=1, tiled=True), w_out, preferre...  3.66 us
  transfers between devices with their start and end apart: 3, of which 3 were waited for; matrix products, arithmetic and copies ran while one was open for 5% of the time, Pallas kernels for 0%

profile of v1, /device:TPU:1, one launch (start us, length us, event | category | flops | bytes accessed | tf_op | source)
XLA Modules:
  0.0 169.6 jit_solution(9894621198003400832)
XLA Ops:
  6.5 0.7 all-gather.3.cloned.1.call-update
  7.3 1.3 multiply_exponential_fusion.2
  8.6 0.7 multiply_exponential_fusion
  9.3 38.8 %all-gather.3.cloned.1.call-done = bf16[512,4096]{1,0:T(8,128)(2,1)} async-done(((bf16[512,512]{1,0:T(8,128)(2,1)}), bf16[512,4096]{1,0:T(8,128)(2,1)}) %all-gather.3.cloned.1.call-update) | async-done | bytes 4194320 | tf_op jit(solution)/shard_map/all_gather | solution.py:16
  48.1 3.2 %multiply_reduce_fusion = f32[512]{0:T(512)S(1)} fusion(bf16[512,4096]{1,0:T(8,128)(2,1)} %all-gather.3.cloned.1.call-done), kind=kLoop, calls=%fused_computation | loop fusion | flops 6290944 | bytes 4196352 | tf_op jit(solution)/shard_map/reduce_sum | solution.py:18
  51.3 0.2 copy-done.1
  51.5 2.9 %fusion.4 = bf16[512,256]{0,1:T(8,128)(2,1)S(1)} fusion(bf16[512,4096]{1,0:T(8,128)(2,1)S(1)} %copy-done.1, bf16[4096,256]{1,0:T(8,128)(2,1)} %param.11, f32[512]{0:T(512)S(1)} %add_rsqrt_fusion), kind=kOutput, calls=%fused_computation.12 | convolution fusion | flops 1074003968 | bytes 6555648 | tf_op jit(solution)/shard_map/dot_general | solution.py:20
  54.5 0.2 copy.15
  54.6 4.2 %multiply_convert_fusion.1 = bf16[512,256]{0,1:T(8,128)(2,1)S(1)} fusion(bf16[512,4096]{1,0:T(8,128)(2,1)} %all-gather.3.cloned.1.call-done, bf16[4096,256]{1,0:T(8,128)(2,1)} %param.10, f32[512]{0:T(512)S(1)} %add_rsqrt_fusion), kind=kOutput, calls=%fused_computation.29 | convolution fusion | flops 1074528256 | bytes 6555648 | tf_op jit(solution)/shard_map/dot_general | solution.py:20
  58.9 0.4 convolution_convert_fusion
  59.3 0.3 copy-done.3
  59.6 1.8 %stack.2 = bf16[32,1,2,128,128]{4,3,2,1,0:T(8,128)(2,1)} broadcast(bf16[2,128,128]{2,1,0:T(8,128)(2,1)S(1)} %convolution_convert_fusion), dimensions={2,3,4} | broadcast | bytes 2162688 | tf_op jit(solution)/shard_map/stack | solution.py:47
  61.5 9.7 %all-to-all-start = ((bf16[32,1,2,128,128]{4,3,2,1,0:T(8,128)(2,1)}), bf16[32,1,2,128,128]{4,3,2,1,0:T(8,128)(2,1)}, u32[]{:S(2)}, u32[]{:S(2)}) async-start(bf16[32,1,2,128,128]{4,3,2,1,0:T(8,128)(2,1)} %stack.2), calls=%async_computation | async-start | bytes 4194304 | tf_op jit(solution)/shard_map/all_to_all | solution.py:46
  71.4 1.0 broadcast_compare_fusion
  72.5 4.9 %multiply_convert_fusion.2 = bf16[512,256]{0,1:T(8,128)(2,1)} fusion(bf16[512,4096]{1,0:T(8,128)(2,1)} %all-gather.3.cloned.1.call-done, bf16[4096,256]{1,0:T(8,128)(2,1)} %param.9, f32[512]{0:T(512)S(1)} %add_rsqrt_fusion), kind=kOutput, calls=%fused_computation.30 | convolution fusion | flops 1074528256 | bytes 6555648 | tf_op jit(solution)/shard_map/dot_general | solution.py:20
  77.5 1.2 copy.14
  78.6 41.5 %all-to-all-done = bf16[32,1,2,128,128]{4,3,2,1,0:T(8,128)(2,1)} async-done(((bf16[32,1,2,128,128]{4,3,2,1,0:T(8,128)(2,1)}), bf16[32,1,2,128,128]{4,3,2,1,0:T(8,128)(2,1)}, u32[]{:S(2)}, u32[]{:S(2)}) %all-to-all-start) | async-done | bytes 2097184 | tf_op jit(solution)/shard_map/all_to_all | solution.py:46
  120.1 2.1 %fusion = f32[2,128,128]{2,1,0:T(8,128)S(1)} fusion(bf16[32,1,2,128,128]{4,3,2,1,0:T(8,128)(2,1)} %all-to-all-done, f32[32,2]{1,0:T(8,128)S(1)} %exponential_select_fusion), kind=kLoop, calls=%fused_computation.2 | loop fusion | flops 3112960 | bytes 2228480 | tf_op jit(solution)/shard_map/reduce_sum | solution.py:61
  122.2 1.6 fusion.12
  123.8 3.0 %multiply_reduce_fusion.1 = (f32[2,512]{1,0:T(2,128)S(1)}, f32[2,512,128]{1,2,0:T(8,128)}) fusion(f32[2,512,128]{1,2,0:T(8,128)} %fusion.12, bf16[2,512,128]{1,2,0:T(8,128)(2,1)} %bitcast.46, bf16[2,512,128]{1,2,0:T(8,128)(2,1)} %bitcast.44, f32[512,512]{1,0:T(8,128)S(1)} %subtract_select_fusion, f32[2]{0:T(128)} %copy-done.7, ...), kind=kOutput, calls=%fused_computation.22 | convolution fusion | flops 270924800 | bytes 3149832 | tf_op jit(solution)/shard_map/hij,hje->hie/dot_general | solution.py:39
  126.8 1.1 bitcast_multiply_fusion.1
  127.9 5.0 %fusion.9 = bf16[512,256]{0,1:T(8,128)(2,1)} fusion(f32[512,2,128]{0,2,1:T(8,128)S(1)} %bitcast_multiply_fusion.1, bf16[512,4096]{1,0:T(8,128)(2,1)} %all-gather.3.cloned.1.call-done, bf16[4096,256]{1,0:T(8,128)(2,1)} %param.12, f32[512]{0:T(512)S(1)} %copy-done.10), kind=kOutput, calls=%fused_computation.20 | convolution fusion | flops 1074659328 | bytes 7079936 | tf_op jit(solution)/shard_map/dot_general | solution.py:20
  132.9 26.2 %all-gather.5.cloned.1.call-done = bf16[512,2048]{0,1:T(8,128)(2,1)} async-done(((bf16[512,256]{0,1:T(8,128)(2,1)}), bf16[512,2048]{0,1:T(8,128)(2,1)}) %all-gather.5.cloned.1.call-update) | async-done | bytes 2097168 | tf_op jit(solution)/shard_map/all_gather | solution.py:73
  159.1 3.7 %fusion.2 = bf16[512,512]{1,0:T(8,128)(2,1)} fusion(bf16[512,2048]{0,1:T(8,128)(2,1)} %all-gather.5.cloned.1.call-done, bf16[2048,512]{1,0:T(8,128)(2,1)S(1)} %copy-done, bf16[512,512]{1,0:T(8,128)(2,1)S(1)} %copy-done.2), kind=kOutput, calls=%fused_computation.6 | convolution fusion | flops 1074528256 | bytes 5242880 | tf_op jit(solution)/shard_map/dot_general | solution.py:72
  (31 shorter events, 0.4 us)
Async XLA Ops:
  6.5 152.5 %copy-start = (bf16[2048,512]{1,0:T(8,128)(2,1)S(1)}, bf16[2048,512]{1,0:T(8,128)(2,1)}, u32[]{:S(2)}) copy-start(bf16[2048,512]{1,0:T(8,128)(2,1)} %param.13) | copy-start | bytes 6291460
  6.5 41.5 %all-gather.3.cloned.1.call-start = ((), (), s32[]{:S(2)}) async-start(), calls=%async_computation.1 | async-start | bytes 4718592 | tf_op jit(solution)/shard_map/all_gather | solution.py:16
  8.6 62.7 %copy-start.7 = (f32[2]{0:T(128)}, f32[2]{0:T(128)S(1)}, u32[]{:S(2)}) copy-start(f32[2]{0:T(128)S(1)} %get-tuple-element.6) | copy-start | bytes 28
  48.1 3.4 %copy-start.1 = (bf16[512,4096]{1,0:T(8,128)(2,1)S(1)}, bf16[512,4096]{1,0:T(8,128)(2,1)}, u32[]{:S(2)}) copy-start(bf16[512,4096]{1,0:T(8,128)(2,1)} %all-gather.3.cloned.1.call-done) | copy-start | bytes 12582916
  51.5 21.0 %copy-start.9 = (f32[512]{0:T(512)}, f32[512]{0:T(512)S(1)}, u32[]{:S(2)}) copy-start(f32[512]{0:T(512)S(1)} %add_rsqrt_fusion) | copy-start | bytes 6148
  54.5 4.4 %copy-start.4 = (bf16[512,256]{0,1:T(8,128)(2,1)}, bf16[512,256]{0,1:T(8,128)(2,1)S(1)}, u32[]{:S(2)}) copy-start(bf16[512,256]{0,1:T(8,128)(2,1)S(1)} %fusion.4) | copy-start | bytes 786436
  58.9 0.7 copy-start.3
  61.5 58.6 %all-to-all-start = ((bf16[32,1,2,128,128]{4,3,2,1,0:T(8,128)(2,1)}), bf16[32,1,2,128,128]{4,3,2,1,0:T(8,128)(2,1)}, u32[]{:S(2)}, u32[]{:S(2)}) async-start(bf16[32,1,2,128,128]{4,3,2,1,0:T(8,128)(2,1)} %stack.2), calls=%async_computation | async-start | bytes 4194304 | tf_op jit(solution)/shard_map/all_to_all | solution.py:46
  71.2 87.9 %all-gather.5.cloned.1.call-start = ((), (), s32[]{:S(2)}) async-start(), calls=%async_computation.2 | async-start | bytes 2359296 | tf_op jit(solution)/shard_map/all_gather | solution.py:73
  77.5 44.7 %copy-start.5 = (f32[2,128,128]{2,1,0:T(8,128)S(1)}, f32[2,128,128]{2,1,0:T(8,128)}, u32[]{:S(2)}) copy-start(f32[2,128,128]{2,1,0:T(8,128)} %param.15) | copy-start | bytes 393220
  120.1 2.1 %copy-start.6 = (f32[2,512]{1,0:T(2,128)S(1)}, f32[2,512]{1,0:T(2,128)}, u32[]{:S(2)}) copy-start(f32[2,512]{1,0:T(2,128)} %get-tuple-element.8) | copy-start | bytes 12292
  120.1 2.1 %copy-start.8 = (f32[2]{0:T(128)S(1)}, f32[2]{0:T(128)}, u32[]{:S(2)}) copy-start(f32[2]{0:T(128)} %get-tuple-element.5) | copy-start | bytes 28
  123.8 4.1 %copy-start.10 = (f32[512]{0:T(512)S(1)}, f32[512]{0:T(512)}, u32[]{:S(2)}) copy-start(f32[512]{0:T(512)} %copy-done.9) | copy-start | bytes 6148
  127.9 31.2 %copy-start.2 = (bf16[512,512]{1,0:T(8,128)(2,1)S(1)}, bf16[512,512]{1,0:T(8,128)(2,1)}, u32[]{:S(2)}) copy-start(bf16[512,512]{1,0:T(8,128)(2,1)} %param.8) | copy-start | bytes 1572868
Sparse Core Ops, SparseCore 0:
  9.2 38.8 all-gather.2
  133.0 25.9 all-gather.4
